TPU v7x, 32 devices: a whole 2x2x4 slice. The times are simulated.
32 devices in a mesh: group: 2 (over y), seq: 4 (over z), head: 4 (over x, core).
Axes of the slice: x: 2, y: 2, z: 4, core: 2. Of those that a mesh axis runs over, the one named last changes fastest.
Arguments:
- tokens: bfloat16 [4096, 768], P(('group', 'seq')), parts along dimension 0, may hold values from -40 to 40
- w_qkv: bfloat16 [3, 768, 768], P(None, None, 'head'), may hold values from -1 to 1
- w_out: bfloat16 [768, 768], P('head'), may hold values from -0.75 to 0.75
- gain: float32 [768], P('head'), may hold values from 0.5 to 1.5
- bias: float32 [768], P('head'), may hold values from -3 to 3
- mid_offset: int32 [12], P('head'), may hold values from 0 to 7
- far_offset: int32 [12], P('head'), may hold values from 0 to 31
Outputs:
- encoded: bfloat16 [4096, 768], P(('group', 'seq'), 'head'), parts along dimension 0
There are 2 independent parts, one for each index of `group`. A program takes and returns all parts, laid end to end along the dimension named above; an argument that names none is the same for every part. Nothing has to cross between parts.
All inputs are finite; a program needn't handle non-finite values.
Results may differ from a plain program's by a relative error of at most 0.0085.
Values may be sent and summed in bfloat16 or wider, within the bound.
No kernel may reach another device: no remote copies, remote signals or barrier semaphores. Data moves between devices by JAX's collectives and lax.ppermute only.
A program may use at most 64 MiB of HBM per device.

v0:
```python
from functools import partial
import math
import jax
import jax.numpy as jnp
from jax import lax
from jax.sharding import PartitionSpec as P

HEADS = 12
SEG0 = 128
R1 = 8
R2 = 32
epsilon = 1e-05


def attend(queries, keys_in, values_in, scale):
    scores = (
        jnp.einsum("qhd,khd->hqk", queries, keys_in, preferred_element_type=jnp.float32) * scale
    )
    peaks = jnp.max(scores, axis=-1)
    shifted = jnp.exp(scores - peaks[..., None])
    masses = jnp.sum(shifted, axis=-1)
    weights = shifted.astype(jnp.bfloat16)
    summed = jnp.einsum("hqk,khd->qhd", weights, values_in, preferred_element_type=jnp.float32)
    result = summed / jnp.transpose(masses)[:, :, None]
    log_mass = jnp.transpose(peaks + jnp.log(masses))
    return (result, log_mass)


def pick(source, offset, rate):
    folded = source.reshape(source.shape[0] // rate, rate, source.shape[1], source.shape[2])
    chosen = lax.broadcasted_iota(jnp.int32, (rate, source.shape[1]), 0) == offset[None, :]
    kept = jnp.where(chosen[None, :, :, None], folded, jnp.zeros((), source.dtype))
    return jnp.sum(kept, axis=1)


def spread(result, log_mass, offset, rate):
    count = result.shape[0]
    chosen = lax.broadcasted_iota(jnp.int32, (rate, result.shape[1]), 0) == offset[None, :]
    full = jnp.where(chosen[None, :, :, None], result[:, None], 0.0)
    full = full.reshape(count * rate, result.shape[1], result.shape[2])
    mass_full = jnp.where(chosen[None], log_mass[:, None, :], -1e30).reshape(
        count * rate, result.shape[1]
    )
    return (full, mass_full)


def local(tokens, w_qkv, w_out, gain, bias, mid_offset, far_offset):
    rows_here = tokens.shape[0]
    width = tokens.shape[1]
    heads_here = mid_offset.shape[0]
    head_size = width // HEADS
    cols_here = heads_here * head_size
    scale = 1.0 / math.sqrt(head_size)
    projected = jnp.einsum("td,sde->ste", tokens, w_qkv, preferred_element_type=jnp.float32).astype(
        jnp.bfloat16
    )
    query = projected[0].reshape(rows_here, heads_here, head_size)
    keyed = projected[1].reshape(rows_here, heads_here, head_size)
    value = projected[2].reshape(rows_here, heads_here, head_size)
    blocks = rows_here // SEG0
    near_out, near_mass = jax.vmap(partial(attend, scale=scale))(
        query.reshape(blocks, SEG0, heads_here, head_size),
        keyed.reshape(blocks, SEG0, heads_here, head_size),
        value.reshape(blocks, SEG0, heads_here, head_size),
    )
    near_out = near_out.reshape(rows_here, heads_here, head_size)
    near_mass = near_mass.reshape(rows_here, heads_here)
    mid_count = rows_here // R1
    far_count = rows_here // R2
    mid_query = pick(query, mid_offset, R1)
    mid_stack = jnp.stack(
        [
            pick(keyed, mid_offset, R1).reshape(mid_count, cols_here),
            pick(value, mid_offset, R1).reshape(mid_count, cols_here),
        ]
    )
    far_query = pick(query, far_offset, R2)
    far_stack = jnp.stack(
        [
            pick(keyed, far_offset, R2).reshape(far_count, cols_here),
            pick(value, far_offset, R2).reshape(far_count, cols_here),
        ]
    )
    mid_devs = min(8, lax.axis_size("seq"))
    place = lax.axis_index("seq")
    gathered_mid, far_all = (
        lax.all_gather(mid_stack, "seq", axis=1, tiled=True),
        lax.all_gather(far_stack, "seq", axis=1, tiled=True),
    )
    first_row = place // mid_devs * (mid_devs * mid_count)
    mid_all = lax.dynamic_slice_in_dim(gathered_mid, first_row, mid_devs * mid_count, 1)
    mid_out, mid_mass = attend(
        mid_query,
        mid_all[0].reshape(-1, heads_here, head_size),
        mid_all[1].reshape(-1, heads_here, head_size),
        scale,
    )
    far_out, far_mass = attend(
        far_query,
        far_all[0].reshape(-1, heads_here, head_size),
        far_all[1].reshape(-1, heads_here, head_size),
        scale,
    )
    mid_full, mid_mfull = spread(mid_out, mid_mass, mid_offset, R1)
    far_full, far_mfull = spread(far_out, far_mass, far_offset, R2)
    top = jnp.maximum(jnp.maximum(near_mass, mid_mfull), far_mfull)
    near_weight = jnp.exp(near_mass - top)
    mid_weight = jnp.exp(mid_mfull - top)
    far_weight = jnp.exp(far_mfull - top)
    mixed = (
        near_weight[..., None] * near_out
        + mid_weight[..., None] * mid_full
        + far_weight[..., None] * far_full
    )
    mixed = mixed / (near_weight + mid_weight + far_weight)[..., None]
    attn = mixed.reshape(rows_here, cols_here).astype(jnp.bfloat16)
    head_count = lax.axis_size("head")
    head_place = lax.axis_index("head")
    piece_cols = width // head_count
    weight_cols = lax.all_to_all(w_out, "head", split_axis=1, concat_axis=0, tiled=True)
    summed = jnp.dot(
        lax.all_gather(attn, "head", axis=1, tiled=True),
        weight_cols,
        preferred_element_type=jnp.float32,
    )
    resid = (
        lax.dynamic_slice_in_dim(tokens, head_place * piece_cols, piece_cols, 1).astype(jnp.float32)
        + summed
    )
    totals, squares = lax.psum((jnp.sum(resid, axis=1), jnp.sum(resid * resid, axis=1)), "head")
    mean = totals / width
    var = squares / width - mean * mean
    normed_cols = (resid - mean[:, None]) * lax.rsqrt(var + epsilon)[:, None]
    return (normed_cols * gain + bias).astype(jnp.bfloat16)


def solution(mesh):
    in_specs = (
        P(("group", "seq"), None),
        P(None, None, "head"),
        P("head", None),
        P("head"),
        P("head"),
        P("head"),
        P("head"),
    )
    out_specs = P(("group", "seq"), "head")
    return jax.shard_map(local, mesh=mesh, in_specs=in_specs, out_specs=out_specs, check_vma=False)
```

profile of v0, /device:TPU:0, one launch (start us, length us, event | category | flops | bytes accessed | tf_op | source)
XLA Modules:
  0.0 76.6 jit_solution(17679054772339913622)
XLA Ops:
  0.0 2.0 %copy.128 = bf16[192,768]{0,1:T(8,128)(2,1)} copy(bf16[192,768]{1,0:T(8,128)(2,1)} %param.9) | data formatting | bytes 589824 | tf_op args[2]
  2.0 4.2 %all-to-all-start = ((bf16[192,4,192]{0,2,1:T(8,128)(2,1)}), bf16[192,4,192]{0,2,1:T(8,128)(2,1)}, u32[]{:S(2)}, u32[]{:S(2)}) async-start(bf16[192,4,192]{0,2,1:T(8,128)(2,1)} %bitcast.24), calls=%async_computation | async-start | bytes 786432 | tf_op jit(solution)/shard_map/all_to_all | solution.py:120
  6.2 0.7 fusion
  7.0 0.1 copy.103
  7.1 0.1 reshape_reshape_squeeze.29
  7.3 0.1 reshape_reshape_squeeze.32
  7.4 0.1 copy.104
  7.7 1.0 %reshape_reshape_squeeze.30 = bf16[64,8,3,64]{3,2,1,0:T(4,128)(2,1)} reshape(bf16[1,512,192]{2,1,0:T(8,128)(2,1)S(1)} %copy.104) | data formatting | bytes 393216 | tf_op jit(solution)/shard_map/reshape;reshape;squeeze | solution.py:30
  8.7 0.1 reshape_reshape_squeeze.33
  8.8 0.1 copy.106
  9.0 0.9 %reshape_reshape_squeeze.31 = bf16[64,8,3,64]{3,2,1,0:T(4,128)(2,1)} reshape(bf16[1,512,192]{2,1,0:T(8,128)(2,1)S(1)} %copy.106) | data formatting | bytes 393216 | tf_op jit(solution)/shard_map/reshape;reshape;squeeze | solution.py:30
  9.9 0.1 reshape_reshape_squeeze.34
  10.1 1.7 %reshape_reshape_squeeze.27 = bf16[4,128,3,64]{1,0,3,2:T(4,128)(2,1)} reshape(bf16[1,512,192]{1,2,0:T(8,128)(2,1)} %copy-done.4) | data formatting | bytes 393216 | tf_op jit(solution)/shard_map/reshape;reshape;squeeze | solution.py:62
  11.8 1.7 %reshape_reshape_squeeze.28 = bf16[4,128,3,64]{1,0,3,2:T(4,128)(2,1)} reshape(bf16[1,512,192]{1,2,0:T(8,128)(2,1)} %copy-done.3) | data formatting | bytes 393216 | tf_op jit(solution)/shard_map/reshape;reshape;squeeze | solution.py:63
  13.4 1.7 %reshape_reshape_squeeze.35 = bf16[4,128,3,64]{1,0,3,2:T(4,128)(2,1)} reshape(bf16[1,512,192]{1,2,0:T(8,128)(2,1)} %copy-done.2) | data formatting | bytes 393216 | tf_op jit(solution)/shard_map/reshape;reshape;squeeze | solution.py:64
  15.1 0.1 copy.102
  15.2 3.4 %select_reduce_fusion.5 = (bf16[64,3,64]{2,1,0:T(4,128)(2,1)}, bf16[64,3,64]{2,1,0:T(4,128)(2,1)}, bf16[64,3,64]{2,1,0:T(4,128)(2,1)}) fusion(bf16[64,8,3,64]{3,2,1,0:T(4,128)(2,1)S(1)} %reshape_reshape_squeeze.29, pred[8,3]{1,0:T(8,128)(4,1)S(1)} %iota_compare_fusion.1, bf16[64,8,3,64]{3,2,1,0:T(4,128)(2,1)S(1)} %copy-done.1, ...), kind=kLoop, calls=%fused_computation.21 | loop fusion | flops 552960 | bytes 663576 | tf_op jit(solution)/shard_map/reduce_sum | solution.py:33
  18.6 0.9 %copy.105 = bf16[64,3,64]{0,2,1:T(8,128)(2,1)S(1)} copy(bf16[64,3,64]{2,1,0:T(4,128)(2,1)} %get-tuple-element.11) | data formatting | bytes 49152 | tf_op jit(solution)/shard_map/reduce_sum | solution.py:33
  19.5 0.9 %copy.107 = bf16[64,3,64]{0,2,1:T(8,128)(2,1)S(1)} copy(bf16[64,3,64]{2,1,0:T(4,128)(2,1)} %get-tuple-element.12) | data formatting | bytes 49152 | tf_op jit(solution)/shard_map/reduce_sum | solution.py:33
  20.5 0.1 copy.108
  20.6 15.6 %all_gather.9 = bf16[2,256,192]{2,0,1:T(2,128)(2,1)S(1)} all-gather(bf16[2,64,192]{2,0,1:T(2,128)(2,1)S(1)} %copy.108), channel_id=1, replica_groups=mesh['group'=2,'seq'=4,'head'=4] {'seq'}, dimensions={1}, use_global_device_ids=true | all-gather | bytes 245760 | tf_op jit(solution)/shard_map/all_gather | solution.py:87
  36.2 0.4 fusion.31
  36.6 0.1 copy.109
  36.8 0.2 fusion.34
  37.0 0.2 fusion.17
  37.3 0.1 broadcast_in_dim.173
  37.4 0.1 copy.111
  37.5 1.1 %select_reduce_fusion.2 = (bf16[16,3,64]{2,1,0:T(4,128)(2,1)S(1)}, bf16[16,3,64]{2,1,0:T(4,128)(2,1)S(1)}, bf16[16,3,64]{2,1,0:T(4,128)(2,1)S(1)}) fusion(bf16[16,32,3,64]{3,2,1,0:T(4,128)(2,1)S(1)} %reshape_reshape_squeeze.32, pred[32,3]{1,0:T(8,128)(4,1)S(1)} %iota_compare_fusion, bf16[16,32,3,64]{3,2,1,0:T(4,128)(2,1)S(1)} %reshape_reshape_squeeze.33, ...), kind=kLoop, calls=%fused_computation.18 | loop fusion | flops 580608 | bytes 608352 | tf_op jit(solution)/shard_map/reduce_sum | solution.py:33
  38.7 0.1 stack_reshape.14
  38.8 0.1 stack_reshape.15
  38.9 13.3 %all_gather.10 = bf16[2,64,192]{2,1,0:T(8,128)(2,1)S(1)} all-gather(bf16[2,16,192]{2,1,0:T(8,128)(2,1)S(1)} %pad_maximum_fusion.1), channel_id=1, replica_groups=mesh['group'=2,'seq'=4,'head'=4] {'seq'}, dimensions={1}, use_global_device_ids=true | all-gather | bytes 61440 | tf_op jit(solution)/shard_map/all_gather | solution.py:88
  52.2 0.1 copy.115
  52.3 0.2 fusion.33
  52.5 0.2 fusion.22
  52.8 0.1 broadcast_in_dim.180
  52.9 0.1 broadcast_in_dim.169
  53.0 0.1 broadcast_in_dim.176
  53.1 0.1 copy.121
  53.3 0.2 fusion.2
  53.5 0.1 copy.122
  53.6 0.1 broadcast_in_dim.183
  53.8 0.6 broadcast_in_dim.184
  54.3 0.2 copy.123
  54.5 0.1 copy.124
  54.6 0.2 fusion.3
  54.9 0.1 broadcast_in_dim.188
  55.0 0.6 broadcast_in_dim.189
  55.6 0.2 copy.127
  55.8 0.2 copy-done.5
  56.0 0.1 copy-done.6
  56.1 0.3 fusion.35
  56.4 0.1 fusion.6
  56.5 0.5 copy-done.8
  57.0 0.3 fusion.1
  57.2 0.3 copy.120
  57.5 1.1 %constant_dynamic-slice_fusion = bf16[512,192]{1,0:T(8,128)(2,1)S(1)} fusion(bf16[512,768]{1,0:T(8,128)(2,1)} %param.7, s32[]{:T(128)S(6)} %select_n.99), kind=kLoop, calls=%fused_computation.61 | loop fusion | bytes 393220 | tf_op jit(solution)/shard_map/dynamic_slice | solution.py:127
  58.6 0.1 copy.133
  58.8 0.2 fusion.12
  59.0 8.8 %all_gather.11 = bf16[512,768]{0,1:T(8,128)(2,1)S(1)} all-gather(bf16[512,192]{0,1:T(8,128)(2,1)S(1)} %fusion.12), channel_id=1, replica_groups=mesh['group'=2,'seq'=4,'head'=4] {'head'}, dimensions={1}, use_global_device_ids=true | all-gather | bytes 983040 | tf_op jit(solution)/shard_map/all_gather | solution.py:122
  67.8 1.3 %copy.129 = bf16[4,192,192]{1,0,2:T(4,128)(2,1)S(1)} copy(bf16[4,192,192]{1,2,0:T(8,128)(2,1)} %bitcast.25) | data formatting | bytes 589824 | tf_op jit(solution)/shard_map/all_to_all | solution.py:120
  69.1 0.3 all_to_all.17
  69.4 0.3 fusion.28
  69.8 6.0 %all-reduce = (f32[512]{0:T(512)S(1)}, f32[512]{0:T(512)S(1)}) all-reduce(f32[512]{0:T(512)S(1)} %get-tuple-element.6, f32[512]{0:T(512)S(1)} %get-tuple-element.5), channel_id=1, replica_groups=mesh['group'=2,'seq'=4,'head'=4] {'head'}, use_global_device_ids=true, to_apply=%region_15.16 | all-reduce | flops 1024 | bytes 8192 | tf_op jit(solution)/shard_map/psum | solution.py:130
  75.8 0.8 %add_convert_fusion = bf16[512,192]{0,1:T(8,128)(2,1)} fusion(f32[512,192]{0,1:T(8,128)S(1)} %get-tuple-element.34, f32[192]{0:T(256)S(1)} %copy-done.10, f32[192]{0:T(256)S(1)} %copy-done.11, f32[512]{0:T(512)S(1)} %get-tuple-element.27, f32[512]{0:T(512)S(1)} %get-tuple-element.26), kind=kLoop, calls=%fused_computation.28 | loop fusion | flops 491520 | bytes 595456 | tf_op jit(solution)/shard_map/convert_element_type | solution.py:134
  (41 shorter events, 0.5 us)
Async XLA Ops:
  0.0 6.2 %copy-start = (bf16[3,768,192]{1,2,0:T(8,128)(2,1)S(1)}, bf16[3,768,192]{1,2,0:T(8,128)(2,1)}, u32[]{:S(2)}) copy-start(bf16[3,768,192]{1,2,0:T(8,128)(2,1)} %param.8) | copy-start | bytes 2654212
  0.0 6.2 %copy-start.9 = (bf16[512,768]{1,0:T(8,128)(2,1)S(1)}, bf16[512,768]{1,0:T(8,128)(2,1)}, u32[]{:S(2)}) copy-start(bf16[512,768]{1,0:T(8,128)(2,1)} %param.7) | copy-start | bytes 2359300
  2.0 65.7 %all-to-all-start = ((bf16[192,4,192]{0,2,1:T(8,128)(2,1)}), bf16[192,4,192]{0,2,1:T(8,128)(2,1)}, u32[]{:S(2)}, u32[]{:S(2)}) async-start(bf16[192,4,192]{0,2,1:T(8,128)(2,1)} %bitcast.24), calls=%async_computation | async-start | bytes 786432 | tf_op jit(solution)/shard_map/all_to_all | solution.py:120
  6.9 0.7 copy-start.3
  7.0 0.7 copy-start.4
  7.0 1.8 %copy-start.2 = (bf16[1,512,192]{1,2,0:T(8,128)(2,1)}, bf16[1,512,192]{1,2,0:T(8,128)(2,1)S(1)}, u32[]{:S(2)}) copy-start(bf16[1,512,192]{1,2,0:T(8,128)(2,1)S(1)} %get-tuple-element.19) | copy-start | bytes 589828
  9.9 5.2 %copy-start.13 = (s32[3]{0:T(128)S(1)}, s32[3]{0:T(128)}, u32[]{:S(2)}) copy-start(s32[3]{0:T(128)} %param.12) | copy-start | bytes 40
  10.0 5.1 %copy-start.1 = (bf16[64,8,3,64]{3,2,1,0:T(4,128)(2,1)S(1)}, bf16[64,8,3,64]{3,2,1,0:T(4,128)(2,1)}, u32[]{:S(2)}) copy-start(bf16[64,8,3,64]{3,2,1,0:T(4,128)(2,1)} %reshape_reshape_squeeze.30) | copy-start | bytes 589828
  20.5 16.3 %copy-start.7 = (bf16[64,3,64]{2,1,0:T(4,128)(2,1)S(1)}, bf16[64,3,64]{2,1,0:T(4,128)(2,1)}, u32[]{:S(2)}) copy-start(bf16[64,3,64]{2,1,0:T(4,128)(2,1)} %get-tuple-element.10) | copy-start | bytes 73732
  36.2 1.2 %copy-start.12 = (s32[3]{0:T(128)S(1)}, s32[3]{0:T(128)}, u32[]{:S(2)}) copy-start(s32[3]{0:T(128)} %param.13) | copy-start | bytes 40
  55.0 0.9 %copy-start.5 = (bf16[4,128,3,64]{1,0,3,2:T(4,128)(2,1)S(1)}, bf16[4,128,3,64]{1,0,3,2:T(4,128)(2,1)}, u32[]{:S(2)}) copy-start(bf16[4,128,3,64]{1,0,3,2:T(4,128)(2,1)} %reshape_reshape_squeeze.27) | copy-start | bytes 589828
  55.0 1.0 %copy-start.6 = (bf16[4,128,3,64]{1,0,3,2:T(4,128)(2,1)S(1)}, bf16[4,128,3,64]{1,0,3,2:T(4,128)(2,1)}, u32[]{:S(2)}) copy-start(bf16[4,128,3,64]{1,0,3,2:T(4,128)(2,1)} %reshape_reshape_squeeze.28) | copy-start | bytes 589828
  56.0 0.9 %copy-start.8 = (bf16[4,128,3,64]{1,0,3,2:T(4,128)(2,1)S(1)}, bf16[4,128,3,64]{1,0,3,2:T(4,128)(2,1)}, u32[]{:S(2)}) copy-start(bf16[4,128,3,64]{1,0,3,2:T(4,128)(2,1)} %reshape_reshape_squeeze.35) | copy-start | bytes 589828
  69.1 6.7 %copy-start.10 = (f32[192]{0:T(256)S(1)}, f32[192]{0:T(256)}, u32[]{:S(2)}) copy-start(f32[192]{0:T(256)} %param.11) | copy-start | bytes 2308
  69.1 6.7 %copy-start.11 = (f32[192]{0:T(256)S(1)}, f32[192]{0:T(256)}, u32[]{:S(2)}) copy-start(f32[192]{0:T(256)} %param.10) | copy-start | bytes 2308
where the time goes:
time: 77.2 us; the launch traced here: 76.6 us
  blocking collectives  43.7 us (57%)
  local copies, waits for them, and re-layouts  19.7 us (26%)
  other arithmetic  6.08 us (8%)
  starting transfers between devices  4.21 us (5%)
  matrix products  2.49 us (3%)
    all_gather x1, blocking collectives, local(): lax.all_gather(mid_stack, 'seq', axis=1, tiled=True)  15.6 us
    all_gather x1, blocking collectives, local(): lax.all_gather(far_stack, 'seq', axis=1, tiled=True)  13.3 us
    all_gather x1, blocking collectives, local(): lax.all_gather(attn, 'head', axis=1, tiled=True)  8.79 us
    psum x1, blocking collectives, local(): lax.psum((jnp.sum(resid, axis=1), jnp.sum(resid * resid, axis=1)), 'head')  6.01 us
    reduce_sum x2, other arithmetic, pick(): return jnp.sum(kept, axis=1)  4.51 us
    all_to_all x1, starting transfers between devices, local(): lax.all_to_all(w_out, 'head', split_axis=1, concat_axis=0, tiled=True)  4.21 us
    unnamed x30, local copies, waits for them, and re-layouts  3.03 us
    another operation x6, local copies, waits for them, and re-layouts, pick(): source.reshape(source.shape[0] // rate, rate, source.shape[1], source.sha...  2.48 us
  transfers between devices with their start and end apart: 1, of which 0 were waited for; matrix products, arithmetic and copies ran while one was open for 29% of the time, Pallas kernels for 0%

commit v1 on v0

--- a/solution.py
+++ b/solution.py
@@ -10,6 +10,27 @@
 R1 = 8
 R2 = 32
 epsilon = 1e-05
+
+
+def ring_gather(x, axis, dim):
+    length, here, extent = (lax.axis_size(axis), lax.axis_index(axis), x.shape[dim])
+    right = [(i, (i + 1) % length) for i in range(length)]
+    downward = [(i, (i - 1) % length) for i in range(length)]
+    filled = jnp.zeros((*x.shape[:dim], length * extent, *x.shape[dim + 1 :]), x.dtype)
+    filled = lax.dynamic_update_slice_in_dim(filled, x, here * extent, axis=dim)
+    from_left = from_right = x
+    halfway = length // 2
+    for step in range(1, halfway + 1):
+        from_left = lax.ppermute(from_left, axis, right)
+        filled = lax.dynamic_update_slice_in_dim(
+            filled, from_left, (here - step) % length * extent, axis=dim
+        )
+        if step < length - halfway:
+            from_right = lax.ppermute(from_right, axis, downward)
+            filled = lax.dynamic_update_slice_in_dim(
+                filled, from_right, (here + step) % length * extent, axis=dim
+            )
+    return filled
 
 
 def attend(queries, keys_in, values_in, scale):
@@ -84,7 +105,7 @@
     mid_devs = min(8, lax.axis_size("seq"))
     place = lax.axis_index("seq")
     gathered_mid, far_all = (
-        lax.all_gather(mid_stack, "seq", axis=1, tiled=True),
+        ring_gather(mid_stack, "seq", 1),
         lax.all_gather(far_stack, "seq", axis=1, tiled=True),
     )
     first_row = place // mid_devs * (mid_devs * mid_count)

time: 77.2 us -> 68.9 us (0.89)
  blocking collectives: 43.7 us -> 28.3 us
  starting transfers between devices: 4.21 us -> 9.38 us
  matrix products: 2.49 us -> 4.38 us
    all_gather x1 -> x0, blocking collectives: 15.6 us -> none  [local(): lax.all_gather(mid_stack, 'seq', axis=1, tiled=True)]
    dynamic_update_slice x0 -> x4, local copies, waits for them, and re-layouts: none -> 5.63 us  [the longest x2 2.78 us: ring_gather(): lax.dynamic_update_slice_in_dim(filled, from_left, (here - step) % length...]
    ppermute x0 -> x3, starting transfers between devices: none -> 5.28 us  [the longest x2 3.25 us: ring_gather(): from_left = lax.ppermute(from_left, axis, right)]
    unnamed x30 -> x26, local copies, waits for them, and re-layouts: 3.03 us -> 5.82 us
    another operation x1, local copies, waits for them, and re-layouts: 1.71 us -> 0.05 us  [local(): query.reshape(blocks, SEG0, heads_here, head_size)]
    another operation x1, local copies, waits for them, and re-layouts: 1.66 us -> 0.05 us  [local(): keyed.reshape(blocks, SEG0, heads_here, head_size)]
    another operation x6, local copies, waits for them, and re-layouts: 2.48 us -> 0.87 us  [pick(): source.reshape(source.shape[0] // rate, rate, source.shape[1], source.sha...]
    another operation x1, local copies, waits for them, and re-layouts: 1.65 us -> 0.05 us  [local(): value.reshape(blocks, SEG0, heads_here, head_size)]
  transfers between devices with their start and end apart: 1 -> 4, of which waited for: 0 -> 0; matrix products, arithmetic and copies ran while one was open for 29% -> 26% of each run, Pallas kernels for 0% -> 0%
where the time goes in v1:
time: 68.9 us; the launch traced here: 68.3 us
  blocking collectives  28.3 us (41%)
  local copies, waits for them, and re-layouts  20.1 us (29%)
  starting transfers between devices  9.38 us (14%)
  other arithmetic  5.56 us (8%)
  matrix products  4.38 us (6%)
    all_gather x1, blocking collectives, local(): lax.all_gather(far_stack, 'seq', axis=1, tiled=True)  13.1 us
    all_gather x1, blocking collectives, local(): lax.all_gather(attn, 'head', axis=1, tiled=True)  9.21 us
    psum x1, blocking collectives, local(): lax.psum((jnp.sum(resid, axis=1), jnp.sum(resid * resid, axis=1)), 'head')  6.01 us
    unnamed x26, local copies, waits for them, and re-layouts  5.82 us
    all_to_all x1, starting transfers between devices, local(): lax.all_to_all(w_out, 'head', split_axis=1, concat_axis=0, tiled=True)  4.1 us
    reduce_sum x2, other arithmetic, pick(): return jnp.sum(kept, axis=1)  3.37 us
    ppermute x2, starting transfers between devices, ring_gather(): from_left = lax.ppermute(from_left, axis, right)  3.25 us
    dynamic_update_slice x2, local copies, waits for them, and re-layouts, ring_gather(): lax.dynamic_update_slice_in_dim(filled, from_left, (here - step) % length...  2.78 us
  transfers between devices with their start and end apart: 4, of which 0 were waited for; matrix products, arithmetic and copies ran while one was open for 26% of the time, Pallas kernels for 0%

profile of v1, /device:TPU:0, one launch (start us, length us, event | category | flops | bytes accessed | tf_op | source)
XLA Modules:
  0.0 68.3 jit_solution(11260870563422977276)
XLA Ops:
  0.0 1.2 %copy-done = bf16[3,768,192]{1,2,0:T(8,128)(2,1)S(1)} copy-done((bf16[3,768,192]{1,2,0:T(8,128)(2,1)S(1)}, bf16[3,768,192]{1,2,0:T(8,128)(2,1)}, u32[]{:S(2)}) %copy-start) | copy-done | bytes 884760
  1.2 1.8 %fusion = bf16[3,512,192]{1,2,0:T(8,128)(2,1)S(1)} fusion(bf16[3,768,192]{1,2,0:T(8,128)(2,1)S(1)} %copy-done, bf16[512,768]{1,0:T(8,128)(2,1)} %param.7), kind=kOutput, calls=%fused_computation.2 | convolution fusion | flops 453279744 | bytes 2260992 | tf_op jit(solution)/shard_map/td,sde->ste/dot_general | solution.py:75
  3.0 0.1 copy.101
  3.2 0.1 reshape_reshape_squeeze.29
  3.3 0.4 copy-done.3
  3.7 0.1 copy.102
  3.8 0.1 reshape_reshape_squeeze.30
  4.0 0.1 copy.104
  4.1 0.1 reshape_reshape_squeeze.31
  4.3 0.2 copy-done.11
  4.5 2.2 %select_reduce_fusion.5 = (bf16[64,3,64]{2,1,0:T(4,128)(2,1)}, bf16[64,3,64]{2,1,0:T(4,128)(2,1)}, bf16[64,3,64]{2,1,0:T(4,128)(2,1)S(1)}) fusion(bf16[64,8,3,64]{3,2,1,0:T(4,128)(2,1)S(1)} %reshape_reshape_squeeze.29, pred[8,3]{1,0:T(8,128)(4,1)S(1)} %iota_compare_fusion.1, bf16[64,8,3,64]{3,2,1,0:T(4,128)(2,1)S(1)} %reshape_reshape_squeeze.30, ...), kind=kLoop, calls=%fused_computation.21 | loop fusion | flops 552960 | bytes 663576 | tf_op jit(solution)/shard_map/reduce_sum | solution.py:54
  6.7 0.9 %copy.103 = bf16[64,3,64]{0,2,1:T(8,128)(2,1)S(1)} copy(bf16[64,3,64]{2,1,0:T(4,128)(2,1)} %get-tuple-element.11) | data formatting | bytes 49152 | tf_op jit(solution)/shard_map/reduce_sum | solution.py:54
  7.7 0.1 copy.105
  7.8 0.7 pad_maximum_fusion
  8.4 3.0 %collective-permute-start = (bf16[2,64,192]{1,2,0:T(8,128)(2,1)}, bf16[2,64,192]{1,2,0:T(8,128)(2,1)}, u32[]{:S(2)}, u32[]{:S(2)}) collective-permute-start(bf16[2,64,192]{1,2,0:T(8,128)(2,1)} %pad_maximum_fusion), channel_id=1, source_target_pairs={{0,4},{4,8},{8,12},{12,0},{1,5},{5,9},{9,13},{13,1},{2,6},{6,10},{... | collective-permute-start | bytes 147464 | tf_op jit(solution)/shard_map/ppermute | solution.py:24
  11.5 2.0 %collective-permute-start.1 = (bf16[2,64,192]{1,2,0:T(8,128)(2,1)}, bf16[2,64,192]{1,2,0:T(8,128)(2,1)}, u32[]{:S(2)}, u32[]{:S(2)}) collective-permute-start(bf16[2,64,192]{1,2,0:T(8,128)(2,1)} %pad_maximum_fusion), channel_id=1, source_target_pairs={{0,12},{4,0},{8,4},{12,8},{1,13},{5,1},{9,5},{13,9},{2,14},{6,2},{... | collective-permute-start | bytes 147464 | tf_op jit(solution)/shard_map/ppermute | solution.py:29
  13.5 1.9 %copy.123 = bf16[192,768]{0,1:T(8,128)(2,1)} copy(bf16[192,768]{1,0:T(8,128)(2,1)} %param.9) | data formatting | bytes 589824 | tf_op args[2]
  15.4 4.1 %all-to-all-start = ((bf16[192,4,192]{0,2,1:T(8,128)(2,1)}), bf16[192,4,192]{0,2,1:T(8,128)(2,1)}, u32[]{:S(2)}, u32[]{:S(2)}) async-start(bf16[192,4,192]{0,2,1:T(8,128)(2,1)} %bitcast.24), calls=%async_computation | async-start | bytes 786432 | tf_op jit(solution)/shard_map/all_to_all | solution.py:141
  19.5 0.1 reshape_reshape_squeeze.32
  19.7 0.1 reshape_reshape_squeeze.33
  19.8 0.1 reshape_reshape_squeeze.34
  20.0 0.4 copy-done.4
  20.5 0.1 copy-done.2
  20.7 1.1 %select_reduce_fusion.2 = (bf16[16,3,64]{2,1,0:T(4,128)(2,1)S(1)}, bf16[16,3,64]{2,1,0:T(4,128)(2,1)S(1)}, bf16[16,3,64]{2,1,0:T(4,128)(2,1)S(1)}) fusion(bf16[16,32,3,64]{3,2,1,0:T(4,128)(2,1)S(1)} %reshape_reshape_squeeze.32, pred[32,3]{1,0:T(8,128)(4,1)S(1)} %iota_compare_fusion, bf16[16,32,3,64]{3,2,1,0:T(4,128)(2,1)S(1)} %reshape_reshape_squeeze.33, ...), kind=kLoop, calls=%fused_computation.18 | loop fusion | flops 580608 | bytes 608352 | tf_op jit(solution)/shard_map/reduce_sum | solution.py:54
  22.1 13.1 %all_gather.6 = bf16[2,64,192]{2,1,0:T(8,128)(2,1)S(1)} all-gather(bf16[2,16,192]{2,1,0:T(8,128)(2,1)S(1)} %pad_maximum_fusion.1), channel_id=1, replica_groups=mesh['group'=2,'seq'=4,'head'=4] {'seq'}, dimensions={1}, use_global_device_ids=true | all-gather | bytes 61440 | tf_op jit(solution)/shard_map/all_gather | solution.py:109
  35.2 0.1 copy.111
  35.3 0.1 copy.119
  35.4 0.2 fusion.33
  35.6 0.2 fusion.22
  35.8 0.3 fusion.35
  36.1 0.1 fusion.6
  36.3 0.2 fusion.3
  36.5 1.0 %fusion.1 = f32[4,128,3,64]{1,3,2,0:T(8,128)} fusion(f32[4,3,128,128]{2,3,1,0:T(8,128)S(1)} %get-tuple-element.33, f32[4,3,128]{2,1,0:T(4,128)S(1)} %get-tuple-element.32, bf16[4,128,3,64]{1,0,3,2:T(4,128)(2,1)S(1)} %reshape_reshape_squeeze.35, f32[4,128,3]{1,2,0:T(4,128)S(1)} %bitcast.120), kind=kOutput, calls=%fused_computation.4 | convolution fusion | flops 25657344 | bytes 1388544 | tf_op jit(solution)/shard_map/vmap(hqk,khd->qhd)/dot_general | solution.py:44
  37.5 0.2 collective-permute-start.2
  37.7 1.1 %constant_dynamic-slice_fusion = bf16[512,192]{1,0:T(8,128)(2,1)S(1)} fusion(bf16[512,768]{1,0:T(8,128)(2,1)} %param.7, s32[]{:T(128)S(6)} %select_n.125), kind=kLoop, calls=%fused_computation.61 | loop fusion | bytes 393220 | tf_op jit(solution)/shard_map/dynamic_slice | solution.py:148
  38.9 0.1 copy.100
  39.0 0.1 copy.107
  39.3 0.1 broadcast_in_dim.172
  39.4 0.1 broadcast_in_dim.180
  39.5 0.1 broadcast_in_dim.192
  39.7 0.6 broadcast_in_dim.193
  40.3 0.2 copy.122
  40.4 0.8 %copy-done.6 = f32[4,128,3,64]{1,3,2,0:T(8,128)S(1)} copy-done((f32[4,128,3,64]{1,3,2,0:T(8,128)S(1)}, f32[4,128,3,64]{1,3,2,0:T(8,128)}, u32[]{:S(2)}) %copy-start.6) | copy-done | bytes 393240
  41.3 0.3 copy.116
  41.5 0.8 %copy.128 = bf16[512,192]{0,1:T(8,128)(2,1)} copy(bf16[512,192]{1,0:T(8,128)(2,1)S(1)} %constant_dynamic-slice_fusion) | data formatting | bytes 393216
  42.3 1.2 %dynamic_update_slice.12 = bf16[2,256,192]{1,2,0:T(8,128)(2,1)S(1)} dynamic-update-slice(bf16[2,256,192]{1,2,0:T(8,128)(2,1)S(1)} %broadcast_in_dim.175, bf16[2,64,192]{1,2,0:T(8,128)(2,1)} %pad_maximum_fusion, s32[]{:T(128)} %constant.58.clone.1, s32[]{:T(128)S(6)} %select_n.129, s32[]{:T(128)} %constant.58.clone.1) | dynamic-update-slice | bytes 98308 | tf_op jit(solution)/shard_map/dynamic_update_slice | solution.py:20
  43.5 1.6 %dynamic_update_slice.13 = bf16[2,256,192]{1,2,0:T(8,128)(2,1)S(1)} dynamic-update-slice(bf16[2,256,192]{1,2,0:T(8,128)(2,1)S(1)} %dynamic_update_slice.12, bf16[2,64,192]{1,2,0:T(8,128)(2,1)} %collective-permute-done, s32[]{:T(128)} %constant.58.clone.1, s32[]{:T(128)S(6)} %select_n.131, s32[]{:T(128)} %constant.58.clone.1) | dynamic-update-slice | bytes 98308 | tf_op jit(solution)/shard_map/dynamic_update_slice | solution.py:25
  45.2 1.7 %dynamic_update_slice.14 = bf16[2,256,192]{1,2,0:T(8,128)(2,1)S(1)} dynamic-update-slice(bf16[2,256,192]{1,2,0:T(8,128)(2,1)S(1)} %dynamic_update_slice.13, bf16[2,64,192]{1,2,0:T(8,128)(2,1)} %collective-permute-done.1, s32[]{:T(128)} %constant.58.clone.1, s32[]{:T(128)S(6)} %select_n.133, s32[]{:T(128)} %constant.58.clone.1) | dynamic-update-slice | bytes 98308 | tf_op jit(solution)/shard_map/dynamic_update_slice | solution.py:30
  46.9 1.2 %dynamic_update_slice.15 = bf16[2,256,192]{1,2,0:T(8,128)(2,1)S(1)} dynamic-update-slice(bf16[2,256,192]{1,2,0:T(8,128)(2,1)S(1)} %dynamic_update_slice.14, bf16[2,64,192]{1,2,0:T(8,128)(2,1)} %collective-permute-done.2, s32[]{:T(128)} %constant.58.clone.1, s32[]{:T(128)S(6)} %select_n.135, s32[]{:T(128)} %constant.58.clone.1) | dynamic-update-slice | bytes 98308 | tf_op jit(solution)/shard_map/dynamic_update_slice | solution.py:25
  48.1 0.2 fusion.34
  48.3 0.2 fusion.17
  48.6 0.1 broadcast_in_dim.177
  48.7 0.2 fusion.2
  49.0 0.1 copy.117
  49.1 0.1 broadcast_in_dim.187
  49.2 0.6 broadcast_in_dim.188
  49.8 0.2 copy.118
  50.0 0.2 fusion.12
  50.2 9.2 %all_gather.7 = bf16[512,768]{0,1:T(8,128)(2,1)S(1)} all-gather(bf16[512,192]{0,1:T(8,128)(2,1)S(1)} %fusion.12), channel_id=1, replica_groups=mesh['group'=2,'seq'=4,'head'=4] {'head'}, dimensions={1}, use_global_device_ids=true | all-gather | bytes 983040 | tf_op jit(solution)/shard_map/all_gather | solution.py:143
  59.4 1.3 %copy.124 = bf16[4,192,192]{1,0,2:T(4,128)(2,1)S(1)} copy(bf16[4,192,192]{1,2,0:T(8,128)(2,1)} %bitcast.25) | data formatting | bytes 589824 | tf_op jit(solution)/shard_map/all_to_all | solution.py:141
  60.7 0.3 all_to_all.17
  61.1 0.3 fusion.28
  61.4 6.0 %all-reduce = (f32[512]{0:T(512)S(1)}, f32[512]{0:T(512)S(1)}) all-reduce(f32[512]{0:T(512)S(1)} %get-tuple-element.6, f32[512]{0:T(512)S(1)} %get-tuple-element.5), channel_id=1, replica_groups=mesh['group'=2,'seq'=4,'head'=4] {'head'}, use_global_device_ids=true, to_apply=%region_15.16 | all-reduce | flops 1024 | bytes 8192 | tf_op jit(solution)/shard_map/psum | solution.py:151
  67.5 0.8 %add_convert_fusion = bf16[512,192]{0,1:T(8,128)(2,1)} fusion(f32[512,192]{0,1:T(8,128)S(1)} %get-tuple-element.34, f32[192]{0:T(256)S(1)} %copy-done.8, f32[192]{0:T(256)S(1)} %copy-done.9, f32[512]{0:T(512)S(1)} %get-tuple-element.27, f32[512]{0:T(512)S(1)} %get-tuple-element.26), kind=kLoop, calls=%fused_computation.28 | loop fusion | flops 491520 | bytes 595456 | tf_op jit(solution)/shard_map/convert_element_type | solution.py:155
  (44 shorter events, 0.8 us)
Async XLA Ops:
  0.0 1.2 %copy-start = (bf16[3,768,192]{1,2,0:T(8,128)(2,1)S(1)}, bf16[3,768,192]{1,2,0:T(8,128)(2,1)}, u32[]{:S(2)}) copy-start(bf16[3,768,192]{1,2,0:T(8,128)(2,1)} %param.8) | copy-start | bytes 2654212
  3.0 0.7 copy-start.3
  3.0 1.0 %copy-start.1 = (bf16[1,512,192]{1,2,0:T(8,128)(2,1)}, bf16[1,512,192]{1,2,0:T(8,128)(2,1)S(1)}, u32[]{:S(2)}) copy-start(bf16[1,512,192]{1,2,0:T(8,128)(2,1)S(1)} %get-tuple-element.20) | copy-start | bytes 589828
  3.8 0.7 copy-start.11
  8.4 29.1 %collective-permute-start = (bf16[2,64,192]{1,2,0:T(8,128)(2,1)}, bf16[2,64,192]{1,2,0:T(8,128)(2,1)}, u32[]{:S(2)}, u32[]{:S(2)}) collective-permute-start(bf16[2,64,192]{1,2,0:T(8,128)(2,1)} %pad_maximum_fusion), channel_id=1, source_target_pairs={{0,4},{4,8},{8,12},{12,0},{1,5},{5,9},{9,13},{13,1},{2,6},{6,10},{... | collective-permute-start | bytes 147464 | tf_op jit(solution)/shard_map/ppermute | solution.py:24
  11.5 33.7 %collective-permute-start.1 = (bf16[2,64,192]{1,2,0:T(8,128)(2,1)}, bf16[2,64,192]{1,2,0:T(8,128)(2,1)}, u32[]{:S(2)}, u32[]{:S(2)}) collective-permute-start(bf16[2,64,192]{1,2,0:T(8,128)(2,1)} %pad_maximum_fusion), channel_id=1, source_target_pairs={{0,12},{4,0},{8,4},{12,8},{1,13},{5,1},{9,5},{13,9},{2,14},{6,2},{... | collective-permute-start | bytes 147464 | tf_op jit(solution)/shard_map/ppermute | solution.py:29
  15.4 44.0 %all-to-all-start = ((bf16[192,4,192]{0,2,1:T(8,128)(2,1)}), bf16[192,4,192]{0,2,1:T(8,128)(2,1)}, u32[]{:S(2)}, u32[]{:S(2)}) async-start(bf16[192,4,192]{0,2,1:T(8,128)(2,1)} %bitcast.24), calls=%async_computation | async-start | bytes 786432 | tf_op jit(solution)/shard_map/all_to_all | solution.py:141
  19.5 0.9 %copy-start.4 = (bf16[1,512,192]{1,2,0:T(8,128)(2,1)S(1)}, bf16[1,512,192]{1,2,0:T(8,128)(2,1)}, u32[]{:S(2)}) copy-start(bf16[1,512,192]{1,2,0:T(8,128)(2,1)} %copy-done.3) | copy-start | bytes 589828
  19.7 1.0 %copy-start.2 = (bf16[1,512,192]{1,2,0:T(8,128)(2,1)S(1)}, bf16[1,512,192]{1,2,0:T(8,128)(2,1)}, u32[]{:S(2)}) copy-start(bf16[1,512,192]{1,2,0:T(8,128)(2,1)} %copy-done.1) | copy-start | bytes 589828
  19.8 0.9 %copy-start.10 = (s32[3]{0:T(128)S(1)}, s32[3]{0:T(128)}, u32[]{:S(2)}) copy-start(s32[3]{0:T(128)} %param.13) | copy-start | bytes 40
  37.5 9.4 %collective-permute-start.2 = (bf16[2,64,192]{1,2,0:T(8,128)(2,1)}, bf16[2,64,192]{1,2,0:T(8,128)(2,1)}, u32[]{:S(2)}, u32[]{:S(2)}) collective-permute-start(bf16[2,64,192]{1,2,0:T(8,128)(2,1)} %collective-permute-done), channel_id=1, source_target_pairs={{0,4},{4,8},{8,12},{12,0},{1,5},{5,9},{9,13},{13,1},{2,6},{6,10},{... | collective-permute-start | bytes 147464 | tf_op jit(solution)/shard_map/ppermute | solution.py:24
  40.3 1.0 %copy-start.6 = (f32[4,128,3,64]{1,3,2,0:T(8,128)S(1)}, f32[4,128,3,64]{1,3,2,0:T(8,128)}, u32[]{:S(2)}) copy-start(f32[4,128,3,64]{1,3,2,0:T(8,128)} %fusion.1) | copy-start | bytes 1179652
  41.5 6.6 %copy-start.7 = (bf16[64,3,64]{2,1,0:T(4,128)(2,1)S(1)}, bf16[64,3,64]{2,1,0:T(4,128)(2,1)}, u32[]{:S(2)}) copy-start(bf16[64,3,64]{2,1,0:T(4,128)(2,1)} %get-tuple-element.10) | copy-start | bytes 73732
  50.2 10.9 %copy-start.5 = (bf16[512,192]{0,1:T(8,128)(2,1)S(1)}, bf16[512,192]{0,1:T(8,128)(2,1)}, u32[]{:S(2)}) copy-start(bf16[512,192]{0,1:T(8,128)(2,1)} %copy.128) | copy-start | bytes 589828
  60.7 6.8 %copy-start.8 = (f32[192]{0:T(256)S(1)}, f32[192]{0:T(256)}, u32[]{:S(2)}) copy-start(f32[192]{0:T(256)} %param.11) | copy-start | bytes 2308
  60.7 6.7 %copy-start.9 = (f32[192]{0:T(256)S(1)}, f32[192]{0:T(256)}, u32[]{:S(2)}) copy-start(f32[192]{0:T(256)} %param.10) | copy-start | bytes 2308
